TPU v7x, 128 devices: a whole 4x4x4 slice. The times are simulated.
128 devices in a mesh: dp: 16 (over x, z_lo, core), tensor: 8 (over z_hi, y).
Axes of the slice: x: 4, y: 4, z: 4 (z_hi: 2, z_lo: 2; z = z_hi * 2 + z_lo), core: 2. Of those that a mesh axis runs over, the one named last changes fastest.
Arguments:
- inputs: bfloat16 [4096, 4096], P('dp', 'tensor'), may hold values from -6 to 6
- gate_pre: bfloat16 [4096, 14336], P('dp', 'tensor'), may hold values from -9 to 9
- up_pre: bfloat16 [4096, 14336], P('dp', 'tensor'), may hold values from -6 to 6
- out_grad: bfloat16 [4096, 4096], P('dp', 'tensor'), may hold values from -0.09375 to 0.09375
- down_weight: bfloat16 [14336, 4096], P('tensor'), may hold values from -0.09375 to 0.09375
Outputs:
- gate_wgrad: bfloat16 [4096, 14336], P('dp', 'tensor')
- up_wgrad: bfloat16 [4096, 14336], P('dp', 'tensor')
- in_cov: float32 [4096, 1024], P(('dp', 'tensor'))
- gate_cov: float32 [8, 1792, 896], P('tensor', 'dp')
- up_cov: float32 [8, 1792, 896], P('tensor', 'dp')
All inputs are finite; a program needn't handle non-finite values.
Results may differ from a plain program's by a relative error of at most 0.014.
Values may be sent and summed in bfloat16 or wider, within the bound.
A program may use at most 192 MiB of HBM per device.

v0:
```python
import jax
import jax.numpy as jnp
from jax import lax
from jax.sharding import PartitionSpec as P

BLK = 1024
HBLK = 896


def sent_together(arrays, axis, dim, along):
    both = jnp.concatenate(arrays, axis=along)
    whole, at, outs = (lax.all_gather(both, axis, axis=dim, tiled=True), 0, [])
    for a in arrays:
        outs.append(lax.slice_in_dim(whole, at, at + a.shape[along], axis=along))
        at += a.shape[along]
    return tuple(outs)


def split_up(x, dim, count):
    shape = x.shape
    tiles = x.reshape(*shape[:dim], count, shape[dim] // count, *shape[dim + 1 :])
    return jnp.moveaxis(tiles, dim, 0)


def summed_on_arrival(x, axis, dim):
    tiles = split_up(x, dim, lax.axis_size(axis))
    arrived = lax.all_to_all(tiles, axis, split_axis=0, concat_axis=0, tiled=True)
    return arrived.astype(jnp.float32).sum(axis=0)


def inner(left, right):
    return lax.dot_general(
        left, right, (((0,), (0,)), ((), ())), preferred_element_type=jnp.float32
    )


def on_device(inputs, gate_pre, up_pre, out_grad, down_weight):
    dp_count = lax.axis_size("dp")
    tp_count = lax.axis_size("tensor")
    dp_index = lax.axis_index("dp")
    tp_index = lax.axis_index("tensor")
    inputs_full, grad_full = sent_together((inputs, out_grad), "tensor", 1, 0)
    tok_rows = inputs_full.shape[0]
    width = inputs_full.shape[1]
    total_tokens = tok_rows * dp_count
    own_width = width // dp_count
    cov_rows = width // (dp_count * tp_count)
    block_count = width // BLK
    repeated = jnp.repeat(
        inputs_full.reshape(tok_rows, block_count, BLK), dp_count // block_count, axis=1
    )
    split = inputs_full.reshape(tok_rows, dp_count, own_width)
    x_owned = lax.all_to_all(split, "dp", split_axis=1, concat_axis=0, tiled=True).reshape(
        total_tokens, own_width
    )
    picked = inputs_full.reshape(tok_rows, dp_count, tp_count, cov_rows)
    picked = lax.dynamic_index_in_dim(picked, tp_index, 2, keepdims=False)
    term = jnp.einsum("tdr,tdb->drb", picked, repeated, preferred_element_type=jnp.float32)
    in_cov = summed_on_arrival(term.astype(jnp.bfloat16), "dp", 0)[0] / total_tokens
    hidden_grad = lax.dot_general(
        grad_full, down_weight, (((1,), (1,)), ((), ())), preferred_element_type=jnp.float32
    )
    gate = gate_pre.astype(jnp.float32)
    up = up_pre.astype(jnp.float32)
    sig = jax.nn.sigmoid(gate)
    gate_grad = (hidden_grad * up * sig * (1.0 + gate * (1.0 - sig))).astype(jnp.bfloat16)
    up_grad = (hidden_grad * gate * sig).astype(jnp.bfloat16)
    hidden = gate_grad.shape[1]
    hid_rows = hidden // dp_count
    row_start = dp_index * hid_rows
    block_start = row_start // HBLK * HBLK

    def accumulate_one(piece):
        wgrad = inner(x_owned, piece)
        own_cols = lax.dynamic_slice_in_dim(piece, row_start, hid_rows, 1)
        block_cols_h = lax.dynamic_slice_in_dim(piece, block_start, HBLK, 1)
        factor = inner(own_cols, block_cols_h)
        return (wgrad, factor)

    gate_sums = accumulate_one(lax.all_gather(gate_grad, "dp", axis=0, tiled=True))
    up_sums = accumulate_one(lax.all_gather(up_grad, "dp", axis=0, tiled=True))
    gate_wgrad = gate_sums[0].astype(jnp.bfloat16)
    up_wgrad = up_sums[0].astype(jnp.bfloat16)
    gate_cov = gate_sums[1].reshape(1, hid_rows, HBLK)
    up_cov = up_sums[1].reshape(1, hid_rows, HBLK)
    return (gate_wgrad, up_wgrad, in_cov, gate_cov, up_cov)


def solution(mesh):
    placed = (
        P("dp", "tensor"),
        P("dp", "tensor"),
        P("dp", "tensor"),
        P("dp", "tensor"),
        P("tensor", None),
    )
    return jax.shard_map(
        on_device,
        mesh=mesh,
        in_specs=placed,
        out_specs=(
            P("dp", "tensor"),
            P("dp", "tensor"),
            P(("dp", "tensor"), None),
            P("tensor", "dp", None),
            P("tensor", "dp", None),
        ),
        check_vma=False,
    )
```

profile of v0, /device:TPU:1, one launch (start us, length us, event | category | flops | bytes accessed | tf_op | source)
XLA Modules:
  0.0 319.3 jit_solution(9122356042220366269)
XLA Ops:
  7.2 0.0 copy-start.4
  7.2 0.0 copy-start.3
  7.2 0.0 all-gather.4.cloned.1.call-start
  7.2 1.2 copy.19
  8.4 1.1 copy.20
  9.5 0.8 pad_maximum_fusion
  10.4 0.0 all-gather.4.cloned.1.call-update
  10.4 0.0 all-gather.6.cloned.1.call-start
  10.4 75.0 %all-gather.4.cloned.1.call-done = bf16[512,4096]{0,1:T(8,128)(2,1)} async-done(((bf16[512,512]{0,1:T(8,128)(2,1)}), bf16[512,4096]{0,1:T(8,128)(2,1)}) %all-gather.4.cloned.1.call-update) | async-done | bytes 4194320 | tf_op jit(solution)/shard_map/all_gather | solution.py:12
  85.4 0.0 copy-done.4
  85.4 0.0 copy-done.3
  85.4 11.7 %fusion.13 = (bf16[256,1792]{1,0:T(8,128)(2,1)}, bf16[256,1792]{1,0:T(8,128)(2,1)}) fusion(bf16[256,1792]{1,0:T(8,128)(2,1)S(1)} %copy-done.3, bf16[256,1792]{1,0:T(8,128)(2,1)S(1)} %copy-done.4, bf16[1792,4096]{1,0:T(8,128)(2,1)} %param.9, bf16[512,4096]{0,1:T(8,128)(2,1)} %all-gather.4.cloned.1.call-done), kind=kOutput, calls=%fused_computation.19 | convolution fusion | flops 3764977664 | bytes 20447232 | tf_op jit(solution)/shard_map/dot_general | solution.py:60
  97.1 0.0 all-gather.6.cloned.1.call-update
  97.1 0.0 all-gather.8.cloned.1.call-start
  97.2 0.7 all-gather.8.cloned.1.call-update
  97.9 3.0 slice.8
  100.9 3.0 copy.22
  103.9 1.1 broadcast_in_dim.3
  105.1 2.5 fusion.14
  107.6 30.8 %all_to_all.20 = bf16[16,1,32,1024]{3,2,1,0:T(8,128)(2,1)S(1)} all-to-all(bf16[16,1,32,1024]{3,2,1,0:T(8,128)(2,1)S(1)} %fusion.14), channel_id=1, replica_groups=mesh['dp'=16,'tensor'=8] {'dp'}, dimensions={0} | all-to-all | bytes 2097152 | tf_op jit(solution)/shard_map/all_to_all | solution.py:27
  138.4 5.1 %all-to-all-start = ((bf16[256,16,256]{0,2,1:T(8,128)(2,1)}), bf16[256,16,256]{0,2,1:T(8,128)(2,1)S(1)}, u32[]{:S(2)}, u32[]{:S(2)}) async-start(bf16[256,16,256]{0,2,1:T(8,128)(2,1)} %bitcast), calls=%async_computation | async-start | bytes 4194304 | tf_op jit(solution)/shard_map/all_to_all | solution.py:53
  143.5 0.2 convert_reduce_fusion
  143.7 0.7 broadcast_multiply_fusion
  144.4 44.8 %all-to-all-done = bf16[256,16,256]{0,2,1:T(8,128)(2,1)S(1)} async-done(((bf16[256,16,256]{0,2,1:T(8,128)(2,1)}), bf16[256,16,256]{0,2,1:T(8,128)(2,1)S(1)}, u32[]{:S(2)}, u32[]{:S(2)}) %all-to-all-start) | async-done | bytes 2097184 | tf_op jit(solution)/shard_map/all_to_all | solution.py:53
  189.2 0.0 copy-start.2
  189.2 1.3 copy-done.2
  190.5 2.9 copy.21
  193.4 17.9 %all-gather.6.cloned.1.call-done = bf16[4096,1792]{1,0:T(8,128)(2,1)} async-done(((bf16[256,1792]{1,0:T(8,128)(2,1)}), bf16[4096,1792]{1,0:T(8,128)(2,1)}) %all-gather.6.cloned.1.call-update) | async-done | bytes 14680080 | tf_op jit(solution)/shard_map/all_gather | solution.py:80
  211.3 8.3 %convolution_convert_fusion.1 = bf16[256,1792]{1,0:T(8,128)(2,1)} fusion(bf16[4096,256]{1,0:T(8,128)(2,1)S(1)} %bitcast.26, bf16[4096,1792]{1,0:T(8,128)(2,1)} %all-gather.6.cloned.1.call-done), kind=kOutput, calls=%fused_computation.8 | convolution fusion | flops 3758555136 | bytes 17694720 | tf_op jit(solution)/shard_map/dot_general | solution.py:32
  219.6 76.5 %all-gather.8.cloned.1.call-done = bf16[4096,1792]{1,0:T(8,128)(2,1)} async-done(((bf16[256,1792]{1,0:T(8,128)(2,1)}), bf16[4096,1792]{1,0:T(8,128)(2,1)}) %all-gather.8.cloned.1.call-update) | async-done | bytes 14680080 | tf_op jit(solution)/shard_map/all_gather | solution.py:81
  296.1 0.0 copy-start
  296.2 0.0 copy-start.1
  296.2 8.5 %convolution_convert_fusion = bf16[256,1792]{1,0:T(8,128)(2,1)} fusion(bf16[4096,256]{1,0:T(8,128)(2,1)S(1)} %bitcast.27, bf16[4096,1792]{1,0:T(8,128)(2,1)} %all-gather.8.cloned.1.call-done), kind=kOutput, calls=%fused_computation.7 | convolution fusion | flops 3758555136 | bytes 17694720 | tf_op jit(solution)/shard_map/dot_general | solution.py:32
  304.6 1.2 copy-done
  305.8 2.6 fusion.15
  308.4 1.7 copy-done.1
  310.2 2.6 fusion.18
Async XLA Ops:
  7.2 78.2 %copy-start.4 = (bf16[256,1792]{1,0:T(8,128)(2,1)S(1)}, bf16[256,1792]{1,0:T(8,128)(2,1)}, u32[]{:S(2)}) copy-start(bf16[256,1792]{1,0:T(8,128)(2,1)} %param.7) | copy-start | bytes 2752516
  7.2 78.2 %copy-start.3 = (bf16[256,1792]{1,0:T(8,128)(2,1)S(1)}, bf16[256,1792]{1,0:T(8,128)(2,1)}, u32[]{:S(2)}) copy-start(bf16[256,1792]{1,0:T(8,128)(2,1)} %param.6) | copy-start | bytes 2752516
  7.2 78.2 %all-gather.4.cloned.1.call-start = ((), (), s32[]{:S(2)}) async-start(), calls=%async_computation.2 | async-start | bytes 4718592 | tf_op jit(solution)/shard_map/all_gather | solution.py:12
  10.4 200.9 %all-gather.6.cloned.1.call-start = ((), (), s32[]{:S(2)}) async-start(), calls=%async_computation.3 | async-start | bytes 15597568 | tf_op jit(solution)/shard_map/all_gather | solution.py:80
  97.1 199.0 %all-gather.8.cloned.1.call-start = ((), (), s32[]{:S(2)}) async-start(), calls=%async_computation.4 | async-start | bytes 15597568 | tf_op jit(solution)/shard_map/all_gather | solution.py:81
  138.4 50.8 %all-to-all-start = ((bf16[256,16,256]{0,2,1:T(8,128)(2,1)}), bf16[256,16,256]{0,2,1:T(8,128)(2,1)S(1)}, u32[]{:S(2)}, u32[]{:S(2)}) async-start(bf16[256,16,256]{0,2,1:T(8,128)(2,1)} %bitcast), calls=%async_computation | async-start | bytes 4194304 | tf_op jit(solution)/shard_map/all_to_all | solution.py:53
  189.2 1.3 copy-start.2
  296.1 9.7 %copy-start = (bf16[4096,1792]{1,0:T(8,128)(2,1)S(1)}, bf16[4096,1792]{1,0:T(8,128)(2,1)}, u32[]{:S(2)}) copy-start(bf16[4096,1792]{1,0:T(8,128)(2,1)} %all-gather.6.cloned.1.call-done) | copy-start | bytes 44040196
  296.2 14.0 %copy-start.1 = (bf16[4096,1792]{1,0:T(8,128)(2,1)S(1)}, bf16[4096,1792]{1,0:T(8,128)(2,1)}, u32[]{:S(2)}) copy-start(bf16[4096,1792]{1,0:T(8,128)(2,1)} %all-gather.8.cloned.1.call-done) | copy-start | bytes 44040196
Sparse Core Ops, SparseCore 0:
  10.9 74.4 all-gather.3
  97.2 114.0 all-gather.5
  213.6 82.5 all-gather.7
where the time goes:
time: 320 us; the launch traced here: 319 us
  waiting for transfers between devices  215 us (67%)
  matrix products  36.2 us (11%)
  blocking collectives  30.8 us (10%)
  local copies, waits for them, and re-layouts  16.6 us (5%)
  between operations  13.8 us (4%)
  starting transfers between devices  5.23 us (2%)
    all_gather x1, waiting for transfers between devices, on_device(): up_sums = accumulate_one(lax.all_gather(up_grad, 'dp', axis=0, tiled=True))  76.5 us
    all_gather x1, waiting for transfers between devices, sent_together(): whole, at, outs = (lax.all_gather(both, axis, axis=dim, tiled=True), 0, [])  75 us
    all_to_all x1, waiting for transfers between devices, on_device(): lax.all_to_all(split, 'dp', split_axis=1, concat_axis=0, tiled=True)  44.8 us
    all_to_all x1, blocking collectives, summed_on_arrival(): lax.all_to_all(tiles, axis, split_axis=0, concat_axis=0, tiled=True)  30.8 us
    dot_general x4, matrix products, inner(): lax.dot_general(left, right, (((0,), (0,)), ((), ())), preferred_element_...  22 us
    all_gather x1, waiting for transfers between devices, on_device(): lax.all_gather(gate_grad, 'dp', axis=0, tiled=True)  17.9 us
    dot_general x1, matrix products, on_device(): lax.dot_general(grad_full, down_weight, (((1,), (1,)), ((), ())), preferr...  11.7 us
    unnamed x12, local copies, waits for them, and re-layouts  6.54 us
  transfers between devices with their start and end apart: 4, of which 4 were waited for; matrix products, arithmetic and copies ran while one was open for 7% of the time, Pallas kernels for 0%

commit v1 on v0

--- a/solution.py
+++ b/solution.py
@@ -77,7 +77,11 @@
         factor = inner(own_cols, block_cols_h)
         return (wgrad, factor)
 
-    gate_sums = accumulate_one(lax.all_gather(gate_grad, "dp", axis=0, tiled=True))
+    gate_sums = accumulate_one(
+        jnp.concatenate(
+            lax.all_to_all(jnp.stack([gate_grad] * lax.axis_size("dp")), "dp", 0, 0), axis=0
+        )
+    )
     up_sums = accumulate_one(lax.all_gather(up_grad, "dp", axis=0, tiled=True))
     gate_wgrad = gate_sums[0].astype(jnp.bfloat16)
     up_wgrad = up_sums[0].astype(jnp.bfloat16)

time: 320 us -> 481 us (1.50)
  waiting for transfers between devices: 215 us -> 313 us
  blocking collectives: 30.8 us -> 83.9 us
  matrix products: 36.2 us -> 42.7 us
    all_to_all x1, waiting for transfers between devices: 44.8 us -> 238 us  [on_device(): lax.all_to_all(jnp.stack([gate_grad] * lax.axis_size('dp')), 'dp', 0, 0)]
    all_gather x1, waiting for transfers between devices: 76.5 us -> 0.01 us  [on_device(): up_sums = accumulate_one(lax.all_gather(up_grad, 'dp', axis=0, tiled=True))]
    all_to_all x0 -> x1, blocking collectives: none -> 53.1 us  [on_device(): lax.all_to_all(split, 'dp', split_axis=1, concat_axis=0, tiled=True)]
    all_gather x1 -> x0, waiting for transfers between devices: 17.9 us -> none  [on_device(): lax.all_gather(gate_grad, 'dp', axis=0, tiled=True)]
    another operation x0 -> x1, local copies, waits for them, and re-layouts: none -> 7.84 us  [on_device(): jnp.stack([gate_grad] * lax.axis_size('dp'))]
    dot_general x4, matrix products: 22 us -> 29.5 us  [inner(): lax.dot_general(left, right, (((0,), (0,)), ((), ())), preferred_element_...]
  transfers between devices with their start and end apart: 4 -> 3, of which waited for: 4 -> 2; matrix products, arithmetic and copies ran while one was open for 7% -> 7% of each run, Pallas kernels for 0% -> 0%
where the time goes in v1:
time: 481 us; the launch traced here: 480 us
  waiting for transfers between devices  313 us (65%)
  blocking collectives  83.9 us (17%)
  matrix products  42.7 us (9%)
  local copies, waits for them, and re-layouts  19.9 us (4%)
  between operations  14.1 us (3%)
  starting transfers between devices  5.2 us (1%)
    all_to_all x1, waiting for transfers between devices, on_device(): lax.all_to_all(jnp.stack([gate_grad] * lax.axis_size('dp')), 'dp', 0, 0)  238 us
    all_gather x1, waiting for transfers between devices, sent_together(): whole, at, outs = (lax.all_gather(both, axis, axis=dim, tiled=True), 0, [])  75 us
    all_to_all x1, blocking collectives, on_device(): lax.all_to_all(split, 'dp', split_axis=1, concat_axis=0, tiled=True)  53.1 us
    all_to_all x1, blocking collectives, summed_on_arrival(): lax.all_to_all(tiles, axis, split_axis=0, concat_axis=0, tiled=True)  30.8 us
    dot_general x4, matrix products, inner(): lax.dot_general(left, right, (((0,), (0,)), ((), ())), preferred_element_...  29.5 us
    dot_general x1, matrix products, on_device(): lax.dot_general(grad_full, down_weight, (((1,), (1,)), ((), ())), preferr...  11.7 us
  transfers between devices with their start and end apart: 3, of which 2 were waited for; matrix products, arithmetic and copies ran while one was open for 7% of the time, Pallas kernels for 0%

profile of v1, /device:TPU:1, one launch (start us, length us, event | category | flops | bytes accessed | tf_op | source)
XLA Modules:
  0.0 480.1 jit_solution(3165291360729129092)
XLA Ops:
  7.2 0.0 copy-start.1
  7.2 0.0 copy-start
  7.2 0.0 all-gather.3.cloned.1.call-start
  7.2 1.2 copy.19
  8.4 1.1 copy.20
  9.5 0.8 pad_maximum_fusion
  10.4 0.0 all-gather.3.cloned.1.call-update
  10.4 0.0 all-gather.5.cloned.1.call-start
  10.4 75.0 %all-gather.3.cloned.1.call-done = bf16[512,4096]{0,1:T(8,128)(2,1)} async-done(((bf16[512,512]{0,1:T(8,128)(2,1)}), bf16[512,4096]{0,1:T(8,128)(2,1)}) %all-gather.3.cloned.1.call-update) | async-done | bytes 4194320 | tf_op jit(solution)/shard_map/all_gather | solution.py:12
  85.4 0.0 copy-done.1
  85.4 0.0 copy-done
  85.4 11.7 %fusion.13 = (bf16[256,1792]{1,0:T(8,128)(2,1)}, bf16[256,1792]{1,0:T(8,128)(2,1)}) fusion(bf16[256,1792]{1,0:T(8,128)(2,1)S(1)} %copy-done, bf16[256,1792]{1,0:T(8,128)(2,1)S(1)} %copy-done.1, bf16[1792,4096]{1,0:T(8,128)(2,1)} %param.9, bf16[512,4096]{0,1:T(8,128)(2,1)} %all-gather.3.cloned.1.call-done), kind=kOutput, calls=%fused_computation.19 | convolution fusion | flops 3764977664 | bytes 20447232 | tf_op jit(solution)/shard_map/dot_general | solution.py:60
  97.1 0.0 all-gather.5.cloned.1.call-update
  97.1 1.7 slice.8
  98.9 2.4 copy.22
  101.3 2.7 broadcast_in_dim.3
  104.0 1.5 fusion.14
  105.6 30.8 %all_to_all.25 = bf16[16,1,32,1024]{3,2,1,0:T(8,128)(2,1)S(1)} all-to-all(bf16[16,1,32,1024]{3,2,1,0:T(8,128)(2,1)S(1)} %fusion.14), channel_id=1, replica_groups=mesh['dp'=16,'tensor'=8] {'dp'}, dimensions={0} | all-to-all | bytes 2097152 | tf_op jit(solution)/shard_map/all_to_all | solution.py:27
  136.4 53.1 %all_to_all.26 = bf16[256,16,256]{0,2,1:T(8,128)(2,1)} all-to-all(bf16[256,16,256]{0,2,1:T(8,128)(2,1)S(1)} %bitcast.31), channel_id=1, replica_groups=mesh['dp'=16,'tensor'=8] {'dp'}, dimensions={1} | all-to-all | bytes 4194304 | tf_op jit(solution)/shard_map/all_to_all | solution.py:53
  189.5 7.8 %stack.2 = bf16[16,256,1792]{2,1,0:T(8,128)(2,1)} broadcast(bf16[256,1792]{1,0:T(8,128)(2,1)} %get-tuple-element.6), dimensions={1,2} | broadcast | bytes 15597568 | tf_op jit(solution)/shard_map/stack | solution.py:82
  197.3 5.1 %all-to-all-start.1 = ((bf16[16,256,1792]{2,1,0:T(8,128)(2,1)}), bf16[16,256,1792]{2,1,0:T(8,128)(2,1)}, u32[]{:S(2)}, u32[]{:S(2)}) async-start(bf16[16,256,1792]{2,1,0:T(8,128)(2,1)} %stack.2), calls=%async_computation.1 | async-start | bytes 29360128 | tf_op jit(solution)/shard_map/all_to_all | solution.py:82
  202.5 0.2 convert_reduce_fusion
  202.7 0.7 broadcast_multiply_fusion
  203.3 2.8 copy.21
  206.2 237.6 %all-to-all-done.1 = bf16[16,256,1792]{2,1,0:T(8,128)(2,1)} async-done(((bf16[16,256,1792]{2,1,0:T(8,128)(2,1)}), bf16[16,256,1792]{2,1,0:T(8,128)(2,1)}, u32[]{:S(2)}, u32[]{:S(2)}) %all-to-all-start.1) | async-done | bytes 14680096 | tf_op jit(solution)/shard_map/all_to_all | solution.py:82
  443.7 6.3 %fusion.15 = f32[1,112,896]{2,1,0:T(8,128)} fusion(bf16[4096,1792]{1,0:T(8,128)(2,1)} %bitcast.4, s32[]{:T(128)S(6)} %select_n.20, s32[]{:T(128)S(6)} %select_n.18), kind=kOutput, calls=%fused_computation.22 | convolution fusion | flops 822083584 | bytes 8790024 | tf_op jit(solution)/shard_map/dot_general | solution.py:32
  450.1 8.3 %convolution_convert_fusion.1 = bf16[256,1792]{1,0:T(8,128)(2,1)} fusion(bf16[4096,256]{1,0:T(8,128)(2,1)S(1)} %bitcast.27, bf16[4096,1792]{1,0:T(8,128)(2,1)} %bitcast.4), kind=kOutput, calls=%fused_computation.8 | convolution fusion | flops 3758555136 | bytes 17694720 | tf_op jit(solution)/shard_map/dot_general | solution.py:32
  458.4 0.0 all-gather.5.cloned.1.call-done
  458.4 6.5 %fusion.18 = f32[1,112,896]{2,1,0:T(8,128)} fusion(bf16[4096,1792]{1,0:T(8,128)(2,1)} %all-gather.5.cloned.1.call-done, s32[]{:T(128)S(6)} %select_n.20, s32[]{:T(128)S(6)} %select_n.18), kind=kOutput, calls=%fused_computation.23 | convolution fusion | flops 822083584 | bytes 8790024 | tf_op jit(solution)/shard_map/dot_general | solution.py:32
  464.9 8.3 %convolution_convert_fusion = bf16[256,1792]{1,0:T(8,128)(2,1)} fusion(bf16[4096,256]{1,0:T(8,128)(2,1)S(1)} %bitcast.28, bf16[4096,1792]{1,0:T(8,128)(2,1)} %all-gather.5.cloned.1.call-done), kind=kOutput, calls=%fused_computation.7 | convolution fusion | flops 3758555136 | bytes 17694720 | tf_op jit(solution)/shard_map/dot_general | solution.py:32
Async XLA Ops:
  7.2 78.2 %copy-start.1 = (bf16[256,1792]{1,0:T(8,128)(2,1)S(1)}, bf16[256,1792]{1,0:T(8,128)(2,1)}, u32[]{:S(2)}) copy-start(bf16[256,1792]{1,0:T(8,128)(2,1)} %param.7) | copy-start | bytes 2752516
  7.2 78.2 %copy-start = (bf16[256,1792]{1,0:T(8,128)(2,1)S(1)}, bf16[256,1792]{1,0:T(8,128)(2,1)}, u32[]{:S(2)}) copy-start(bf16[256,1792]{1,0:T(8,128)(2,1)} %param.6) | copy-start | bytes 2752516
  7.2 78.2 %all-gather.3.cloned.1.call-start = ((), (), s32[]{:S(2)}) async-start(), calls=%async_computation.3 | async-start | bytes 4718592 | tf_op jit(solution)/shard_map/all_gather | solution.py:12
  10.4 448.0 %all-gather.5.cloned.1.call-start = ((), (), s32[]{:S(2)}) async-start(), calls=%async_computation.4 | async-start | bytes 15597568 | tf_op jit(solution)/shard_map/all_gather | solution.py:85
  197.3 246.4 %all-to-all-start.1 = ((bf16[16,256,1792]{2,1,0:T(8,128)(2,1)}), bf16[16,256,1792]{2,1,0:T(8,128)(2,1)}, u32[]{:S(2)}, u32[]{:S(2)}) async-start(bf16[16,256,1792]{2,1,0:T(8,128)(2,1)} %stack.2), calls=%async_computation.1 | async-start | bytes 29360128 | tf_op jit(solution)/shard_map/all_to_all | solution.py:82
Sparse Core Ops, SparseCore 0:
  10.9 74.4 all-gather.2
  97.2 117.9 all-gather.4
